TPU v7x, 512 devices: a whole 4x4x16 slice. The times are simulated.
512 devices in a mesh: wide: 128 (over z, y, core), pair: 4 (over x).
Axes of the slice: x: 4, y: 4, z: 16, core: 2. Of those that a mesh axis runs over, the one named last changes fastest.
Arguments:
- three_center: bfloat16 [512, 8, 1024], P('wide'), may hold values from -0.3125 to 0.3125
- occ_green: bfloat16 [512, 128, 8, 8], P('wide', 'pair'), may hold values from -2 to 2
- virt_green: bfloat16 [512, 128, 8, 8], P('wide', 'pair'), may hold values from -2 to 2
- occ_column: int32 [512, 128], P('wide', 'pair'), may hold values from 0 to 511, as said below
- partner_live: int32 [512, 128], P('wide', 'pair'), may hold values 0 or 1
Outputs:
- response: float32 [128, 128], P('pair')
Inputs may be any that keep to these rules, and one draw needn't show every extreme that they name: `occ_column`: for each index of pair and each index w of wide, the slots of that group on the 4 atom blocks w * 4 to w * 4 + 3 name partner blocks k such that no value of k // 4 occurs more than 2 times, and some value occurs exactly 2 times.
All inputs are finite; a program needn't handle non-finite values. No bound on the sum of `partner_live` on one device may be relied on, other than what follows from the above.
Results may differ from a plain program's by a relative error of at most 0.004.
Values may be sent and summed in bfloat16 or wider, within the bound.
A program may use at most 64 MiB of HBM per device.

v0:
```python
import jax
import jax.numpy as jnp
from jax import lax
from jax.sharding import PartitionSpec as P

CAP = 2


def apply_virtual(occupied, virt_blocks, block_size):
    shaped = occupied.reshape(occupied.shape[:-1] + (block_size, -1))
    product = jnp.einsum(
        "...lnp,...ns->...lsp", shaped, virt_blocks, preferred_element_type=jnp.float32
    )
    return product.astype(jnp.bfloat16).reshape(occupied.shape)


def slot_ranks(owners):
    unit_count = owners.shape[-1]
    same_owner = owners[..., :, None] == owners[..., None, :]
    before = jnp.arange(unit_count)[None, :] < jnp.arange(unit_count)[:, None]
    return jnp.sum(same_owner & before, axis=-1)


def local(three_center, occ_green, virt_green, occ_column, partner_live):
    local_atoms, block_size, wide_row = three_center.shape
    aux_count = wide_row // block_size
    wide_count = lax.axis_size("wide")
    slot_total = wide_count * CAP
    unit_count = occ_green.shape[0] * occ_green.shape[1]
    listed = lax.all_gather(occ_column, "wide", axis=0, tiled=True).reshape(wide_count, unit_count)
    listed_owner = listed // local_atoms
    listed_rank = slot_ranks(listed_owner)
    to_here = listed_owner == lax.axis_index("wide")
    chosen = to_here[:, None, :] & (listed_rank[:, None, :] == jnp.arange(CAP)[None, :, None])
    slot_atom = jnp.sum(jnp.where(chosen, (listed % local_atoms)[:, None, :], 0), axis=2).reshape(
        slot_total
    )
    slot_used = jnp.any(chosen, axis=2).reshape(slot_total)
    occupied = jnp.einsum(
        "amnl,anx->amlx", occ_green, three_center, preferred_element_type=jnp.float32
    )
    occupied = occupied * partner_live.astype(jnp.float32)[:, :, None, None]
    occupied = occupied.astype(jnp.bfloat16).reshape(unit_count, block_size, wide_row)
    owners = (occ_column // local_atoms).reshape(unit_count)
    position = owners * CAP + slot_ranks(owners)
    virt_units = virt_green.reshape(unit_count, block_size, block_size)
    own_rows = three_center.astype(jnp.float32).reshape(-1, aux_count)
    both = apply_virtual(occupied, virt_units, block_size)
    outgoing = jnp.zeros((slot_total, block_size, wide_row), jnp.bfloat16).at[position].set(both)
    arrived = lax.all_to_all(
        outgoing.reshape(wide_count, CAP, block_size, wide_row),
        "wide",
        split_axis=0,
        concat_axis=0,
        tiled=True,
    )
    routing = (
        (slot_atom[None, :] == jnp.arange(local_atoms)[:, None]) & slot_used[None, :]
    ).astype(jnp.bfloat16)
    partner_sum = jnp.dot(
        routing, arrived.reshape(slot_total, -1), preferred_element_type=jnp.float32
    )
    partner_rows = partner_sum.reshape(-1, aux_count)
    response_part = lax.dot_general(
        partner_rows,
        own_rows,
        (((0,), (0,)), ((), ())),
        precision=lax.Precision.HIGHEST,
        preferred_element_type=jnp.float32,
    )
    total = lax.psum(response_part, ("wide", "pair"))
    row_count = aux_count // lax.axis_size("pair")
    result = lax.dynamic_slice_in_dim(total, lax.axis_index("pair") * row_count, row_count, 0)
    return result


def solution(mesh):
    placed = (
        P("wide", None, None),
        P("wide", "pair", None, None),
        P("wide", "pair", None, None),
        P("wide", "pair"),
        P("wide", "pair"),
    )
    return jax.shard_map(
        local, mesh=mesh, in_specs=placed, out_specs=P("pair", None), check_vma=False
    )
```

profile of v0, /device:TPU:1, one launch (start us, length us, event | category | flops | bytes accessed | tf_op | source)
XLA Modules:
  0.0 793.3 jit_solution(15315771442357756404)
XLA Ops:
  6.5 0.7 broadcast_multiply_fusion
  7.4 0.2 convert_reduce_fusion.1
  7.6 1.1 copy.39
  8.7 1.1 copy.33
  9.8 0.7 convert_element_type.22
  10.5 1.5 multiply_convert_fusion
  12.0 2.0 convert_bitcast_fusion
  14.1 2.8 reshape.166
  16.9 2.5 broadcast_in_dim.12
  19.4 15.7 %scatter_fusion = bf16[256,8,1024]{2,1,0:T(8,128)(2,1)} fusion(bf16[256,8,1024]{2,1,0:T(8,128)(2,1)} %broadcast_in_dim.12, s32[128]{0:T(128)S(1)} %fusion.17, bf16[128,8,1024]{2,1,0:T(8,128)(2,1)S(1)} %reshape.166), kind=kCustom, calls=%fused_computation | custom fusion | bytes 6291968 | tf_op jit(solution)/shard_map/scatter | solution.py:49
  35.1 21.2 %all-to-all-start = ((bf16[128,2,8,1024]{3,2,1,0:T(8,128)(2,1)}), bf16[128,2,8,1024]{3,2,1,0:T(8,128)(2,1)}, u32[]{:S(2)}, u32[]{:S(2)}) async-start(bf16[128,2,8,1024]{3,2,1,0:T(8,128)(2,1)} %bitcast.58), calls=%async_computation | async-start | bytes 8388608 | tf_op jit(solution)/shard_map/all_to_all | solution.py:50
  56.4 276.5 %all-gather = s32[128,4,32]{2,1,0:T(4,128)S(1)} all-gather(s32[1,4,32]{2,1,0:T(4,128)S(1)} %bitcast.62), channel_id=1, replica_groups=mesh['wide'=128,'pair'=4] {'wide'}, dimensions={0}, use_global_device_ids=true | all-gather | bytes 66048 | tf_op jit(solution)/shard_map/all_gather | solution.py:30
  333.3 0.1 copy.27
  333.5 5.1 convert_reduce_fusion
  338.7 0.1 copy.31
  338.8 0.1 eq.76
  339.0 0.1 fusion.5
  339.1 0.1 copy.32
  339.2 0.2 and.81
  339.4 6.5 copy.41
  345.9 0.7 fusion.11
  346.7 0.9 fusion.18
  347.6 437.5 %all-reduce.2.cloned.1.call-done = f32[128,128]{1,0:T(8,128)} async-done(((f32[128,128]{1,0:T(8,128)}), f32[128,128]{1,0:T(8,128)}) %all-reduce.2.cloned.1.call-update) | async-done | bytes 65552 | tf_op jit(solution)/shard_map/psum | solution.py:71
  785.1 1.3 constant_dynamic-slice_fusion
  (19 shorter events, 0.9 us)
Async XLA Ops:
  35.1 21.2 %copy-start = (bf16[4,8,1024]{2,1,0:T(8,128)(2,1)S(1)}, bf16[4,8,1024]{2,1,0:T(8,128)(2,1)}, u32[]{:S(2)}) copy-start(bf16[4,8,1024]{2,1,0:T(8,128)(2,1)} %param.5) | copy-start | bytes 196612
  35.1 21.3 %copy-start.1 = (s32[4,32]{1,0:T(4,128)S(1)}, s32[4,32]{1,0:T(4,128)}, u32[]{:S(2)}) copy-start(s32[4,32]{1,0:T(4,128)} %param.8) | copy-start | bytes 1540
  35.1 304.3 %all-to-all-start = ((bf16[128,2,8,1024]{3,2,1,0:T(8,128)(2,1)}), bf16[128,2,8,1024]{3,2,1,0:T(8,128)(2,1)}, u32[]{:S(2)}, u32[]{:S(2)}) async-start(bf16[128,2,8,1024]{3,2,1,0:T(8,128)(2,1)} %bitcast.58), calls=%async_computation | async-start | bytes 8388608 | tf_op jit(solution)/shard_map/all_to_all | solution.py:50
  56.3 728.9 %all-reduce.2.cloned.1.call-start = ((), (), s32[]{:S(2)}) async-start(), calls=%async_computation.1 | async-start | bytes 131072 | tf_op jit(solution)/shard_map/psum | solution.py:71
Sparse Core Ops, SparseCore 0:
  347.7 437.3 all-reduce.1
where the time goes:
time: 794 us; the launch traced here: 793 us
  waiting for transfers between devices  438 us (55%)
  blocking collectives  277 us (35%)
  local copies, waits for them, and re-layouts  32.3 us (4%)
  starting transfers between devices  21.2 us (3%)
  between operations  13.6 us (2%)
    psum x1, waiting for transfers between devices, local(): total = lax.psum(response_part, ('wide', 'pair'))  438 us
    all_gather x1, blocking collectives, local(): lax.all_gather(occ_column, 'wide', axis=0, tiled=True)  277 us
    all_to_all x1, starting transfers between devices, local(): lax.all_to_all(outgoing.reshape(wide_count, CAP, block_size, wide_row), '...  21.2 us
  transfers between devices with their start and end apart: 2, of which 1 were waited for; matrix products, arithmetic and copies ran while one was open for 1% of the time, Pallas kernels for 0%

commit v1 on v0

v1 whole, which is shorter than its diff:
```python
import jax
import jax.numpy as jnp
from jax import lax
from jax.experimental import pallas as pl
from jax.experimental.pallas import tpu as pltpu
from jax.sharding import PartitionSpec as P

NZ, NY, NC, NX = 16, 4, 2, 4
PEERS = NX * NY
OWN = 8
CAP = 2
AD = 4
BB = 64
PB = 128
MESH = pl.DeviceIdType.MESH
F32 = jnp.float32
BF16 = jnp.bfloat16
NT = (((1,), (1,)), ((), ()))
TN = (((0,), (0,)), ((), ()))


def iota(shape, dim):
    return lax.broadcasted_iota(jnp.int32, shape, dim)


def one_hot(cond):
    return jnp.where(cond, 1.0, 0.0)


def kernel(
    t_ref, occ_ref, virt_ref, col_ref, live_ref, out_ref,
    sbuf, rbuf, ta, tk, meta_v, meta_s, oo, vv, lhs, rhs, yb, r3, g1, mine, g2, fin, g3,
    u_send, u_recv, a_send, a_recv, ka_send, kb_send, kc_send, k_recv, kc_recv,
    p1_send, p1_recv, p2_send, p2_recv, p3_send, p3_recv, loc,
):
    w = lax.axis_index("wide")
    x = lax.axis_index("pair")
    z = w // (NY * NC)
    y = (w // NC) % NY
    c = w % NC

    def place(zz, yy, cc):
        return zz * (NY * NC) + yy * NC + cc

    def remote(src, dst, ss, rs, wide, pair):
        return pltpu.make_async_remote_copy(
            src_ref=src, dst_ref=dst, send_sem=ss, recv_sem=rs, device_id=(wide, pair), device_id_type=MESH
        )

    barrier = pltpu.get_barrier_semaphore()
    for dx in range(NX):
        for dy in range(NY):
            for dc in range(NC):
                if dx + dy + dc:
                    pl.semaphore_signal(
                        barrier, inc=1, device_id_type=MESH,
                        device_id=(place(z, (y + dy) % NY, (c + dc) % NC), (x + dx) % NX),
                    )
    for dz in range(1, NZ):
        pl.semaphore_signal(
            barrier, inc=1, device_id_type=MESH, device_id=(place((z + dz) % NZ, y, c), x)
        )

    own_ta = pltpu.make_async_copy(t_ref, ta.at[pl.ds(0, AD * BB)], loc.at[0])
    own_ta.start()

    tri = one_hot(iota((32, 32), 0) < iota((32, 32), 1)).astype(BF16)
    base = jnp.zeros((PEERS * OWN, 1), F32)
    packed = jnp.zeros((PEERS * OWN * CAP, PB), F32)
    codes = jnp.zeros((PEERS, PB), F32)
    for a in range(AD):
        k = col_ref[a : a + 1, :]
        owner = k // AD
        zk, yk, ck = owner // (NY * NC), (owner // NC) % NY, owner % NC
        dest = (zk % NX) * NY + yk
        ow = (zk // NX) * NC + ck
        hit = one_hot(iota((PEERS * OWN, 32), 0) == dest * OWN + ow)
        hit16 = hit.astype(BF16)
        before = jnp.dot(hit16, tri, preferred_element_type=F32) + base
        base = base + jnp.sum(hit, axis=1, keepdims=True)
        rank = jnp.sum(hit * before, axis=0, keepdims=True).astype(jnp.int32)
        inner = rank * OWN + ow
        take = (iota((PEERS * OWN * CAP, 32), 0) == dest * (OWN * CAP) + inner) & (live_ref[a : a + 1, :] > 0)
        units = jnp.concatenate([occ_ref[a], virt_ref[a]], axis=0)
        packed += lax.dot_general(one_hot(take).astype(BF16), units, NT, preferred_element_type=F32)
        code = jnp.where(iota((PEERS, 32), 0) == dest, (a * AD + k % AD).astype(F32), 0.0).astype(BF16)
        spot = one_hot(iota((PB, 32), 0) == inner).astype(BF16)
        codes += lax.dot_general(code, spot, NT, preferred_element_type=F32)
    for j in range(PEERS):
        sbuf[j, 0:16, :] = packed[j * 16 : (j + 1) * 16].astype(BF16)
        sbuf[j, 16:32, :] = jnp.broadcast_to(codes[j : j + 1], (16, PB)).astype(BF16)

    pl.semaphore_wait(barrier, PEERS * NC - 1 + NZ - 1)

    offsets = [(dx, dy) for dx in range(NX) for dy in range(NY)]
    sends = []
    for d, (dx, dy) in enumerate(offsets):
        if d:
            xt, yt = (x + dx) % NX, (y + dy) % NY
            copy = remote(sbuf.at[xt * NY + yt], rbuf.at[d], u_send.at[d], u_recv.at[d], place(z, yt, c), xt)
            copy.start()
            sends.append(copy)
    own_units = pltpu.make_async_copy(sbuf.at[x * NY + y], rbuf.at[0], loc.at[1])
    own_units.start()

    arrivals = []
    for dy in range(1, NY):
        copy = remote(
            t_ref, ta.at[pl.ds(dy * AD * BB, AD * BB)], a_send.at[dy], a_recv.at[dy], place(z, (y + dy) % NY, c), x
        )
        copy.start()
        arrivals.append(copy)
        sends.append(copy)

    phase = (z + NZ - x) % NX
    source = (z + NZ - jnp.where(phase == 3, -1, phase)) % NZ
    qs = source // NX

    def spread(i, src, to_z):
        row = ((qs + NX - i) % NX) * NC + c
        if to_z:
            for n, dz in enumerate((1, NZ - 1, 2)):
                remote(
                    src, tk.at[row], kb_send.at[i * 3 + n], k_recv.at[i], place((z + dz) % NZ, y, c), x
                ).start()
        remote(src, tk.at[row], kc_send.at[i], kc_recv.at[i], place(z, y, 1 - c), x).start()

    def block(i):
        return tk.at[((qs + NX - i) % NX) * NC + c]

    def other(i):
        return tk.at[((qs + NX - i) % NX) * NC + 1 - c]

    own_tk = pltpu.make_async_copy(t_ref, block(0), loc.at[2])

    @pl.when(phase == 0)
    def _():
        own_tk.start()
        for i in range(1, NX):
            remote(t_ref, block(0), ka_send.at[i], k_recv.at[i], place((z + NX * i) % NZ, y, c), x).start()
        spread(0, t_ref, True)

    own_units.wait()
    for d in range(1, PEERS):
        remote(sbuf.at[0], rbuf.at[d], u_send.at[d], u_recv.at[d], w, x).wait_recv()
    for d in range(PEERS):
        meta_v[d : d + 1, :] = rbuf[d, 16:17, :].astype(F32).astype(jnp.int32)
    to_smem = pltpu.make_async_copy(meta_v, meta_s, loc.at[3])
    to_smem.start()
    got = rbuf[:, 0:16, :].astype(F32).reshape(PEERS, CAP, OWN, PB)
    both = jnp.concatenate(
        [got[:, 0].reshape(PEERS * OWN, PB).astype(BF16), got[:, 1].reshape(PEERS * OWN, PB).astype(BF16)], axis=1
    )
    row = iota((CAP * PB, PB), 0)
    lane = iota((CAP * PB, PB), 1)
    for f, arr in enumerate((oo, vv)):
        pick = (lane % 8) if f == 0 else (lane // 8) % 8
        target = (lane // BB) * PB + f * BB + pick * 8
        for g in range(8):
            sel = one_hot(row == target + g).astype(BF16)
            arr[:, g, :] = jnp.dot(both, sel, preferred_element_type=F32)
    to_smem.wait()

    @pl.when(phase == 0)
    def _():
        for i in range(1, NX):
            remote(t_ref, block(i), ka_send.at[i], k_recv.at[i], w, x).wait_recv()
            spread(i, block(i), True)

    own_ta.wait()
    for copy in arrivals:
        copy.wait_recv()

    def one_owner(ow, carry):
        low = iota((8, PB), 1) < BB
        for d, (dx, dy) in enumerate(offsets):
            c0, c1 = meta_s[d, ow], meta_s[d, OWN + ow]
            kv = jnp.where(low, c0 & 3, c1 & 3)
            o = oo[d * OWN + ow]
            v = vv[d * OWN + ow]
            vs = [jnp.broadcast_to(v[s : s + 1, :], (8, PB)) for s in range(8)]
            for kk in range(AD):
                ok = jnp.where(kv == kk, o, 0.0)
                for s in range(0, 8, 2):
                    m = jnp.concatenate([ok * vs[s], ok * vs[s + 1]], axis=0).astype(BF16)
                    lhs[kk * BB + s * 8 : kk * BB + s * 8 + 16, d * PB : (d + 1) * PB] = m
            for cap, code in ((0, c0), (1, c1)):
                atoms = [ta[(dy * AD + a) * BB : (dy * AD + a + 1) * BB, :] for a in range(AD)]
                low_pair = jnp.where((code & 4) == 0, atoms[0], atoms[1])
                high_pair = jnp.where((code & 4) == 0, atoms[2], atoms[3])
                rhs[d * PB + cap * BB : d * PB + (cap + 1) * BB, :] = jnp.where(
                    (code & 8) == 0, low_pair, high_pair
                )
        yb[pl.ds(pl.multiple_of(ow * AD * BB, AD * BB), AD * BB), :] = jnp.dot(
            lhs[...], rhs[...], preferred_element_type=F32
        )
        return carry

    lax.fori_loop(0, OWN // 2, one_owner, 0)

    @pl.when(phase != 0)
    def _():
        for i in range(NX):
            remote(t_ref, block(i), ka_send.at[i], k_recv.at[i], w, x).wait_recv()
            spread(i, block(i), False)

    lax.fori_loop(OWN // 2, OWN, one_owner, 0)

    @pl.when(phase == 0)
    def _():
        own_tk.wait()

    for i in range(NX):
        remote(t_ref, other(i), kc_send.at[i], kc_recv.at[i], w, x).wait_recv()

    total = jnp.zeros((2 * PB, PB), F32)
    for ow in range(OWN):
        yy = yb[ow * AD * BB : (ow + 1) * AD * BB, :]
        hi = yy.astype(BF16)
        lo = (yy - hi.astype(F32)).astype(BF16)
        total += lax.dot_general(
            jnp.concatenate([hi, lo], axis=1), tk[ow], TN, preferred_element_type=F32
        )
    part = total[:PB] + total[PB:]
    for xx in range(NX):
        for n in range(NY * NC):
            r3[xx, n] = part[xx * 32 + n * 4 : xx * 32 + n * 4 + 4]

    waits = []
    d = 0
    for dx in range(NX):
        for dy in range(NY):
            for dc in range(NC):
                if d:
                    xt, yt, ct = (x + dx) % NX, (y + dy) % NY, (c + dc) % NC
                    copy = remote(
                        r3.at[xt, yt * NC + ct], g1.at[d], p1_send.at[d], p1_recv.at[d], place(z, yt, ct), xt
                    )
                    copy.start()
                    waits.append(copy)
                d += 1
    total4 = r3[x, y * NC + c]
    for copy in waits:
        copy.wait_recv()
    sends += waits
    for d in range(1, PEERS * NC):
        total4 += g1[d]
    mine[...] = total4

    waits = []
    for dz in range(1, NZ):
        copy = remote(mine, g2.at[z], p2_send.at[dz], p2_recv.at[dz], place((z + dz) % NZ, y, c), x)
        copy.start()
        waits.append(copy)
    g2[z] = total4
    for copy in waits:
        copy.wait_recv()
    sends += waits
    total4 = g2[0]
    for n in range(1, NZ):
        total4 += g2[n]
    fin[...] = total4

    waits = []
    here = y * NC + c
    for n in range(1, NY * NC):
        dy, dc = n // NC, n % NC
        copy = remote(
            fin, g3.at[here], p3_send.at[n], p3_recv.at[n], place(z, (y + dy) % NY, (c + dc) % NC), x
        )
        copy.start()
        waits.append(copy)
    g3[here] = total4
    for copy in waits:
        copy.wait_recv()
    sends += waits
    for n in range(NY * NC):
        out_ref[n * 4 : (n + 1) * 4, :] = g3[n]

    for copy in sends:
        copy.wait_send()
    for i in range(NX):
        remote(t_ref, block(i), kc_send.at[i], kc_recv.at[i], w, x).wait_send()

    @pl.when(phase == 0)
    def _():
        for i in range(1, NX):
            remote(t_ref, block(i), ka_send.at[i], k_recv.at[i], w, x).wait_send()
        for i in range(3 * NX):
            remote(t_ref, block(0), kb_send.at[i], k_recv.at[0], w, x).wait_send()


def local(three_center, occ_green, virt_green, occ_column, partner_live):
    t = three_center.reshape(AD, 8, 8, PB).transpose(0, 2, 1, 3).reshape(AD * BB, PB)
    occ = occ_green.transpose(0, 2, 3, 1).reshape(AD, BB, 32)
    virt = virt_green.transpose(0, 2, 3, 1).reshape(AD, BB, 32)
    vmem = pl.BlockSpec(memory_space=pltpu.VMEM)
    dma = pltpu.SemaphoreType.DMA
    return pl.pallas_call(
        kernel,
        out_shape=jax.ShapeDtypeStruct((32, PB), F32),
        in_specs=[vmem] * 5,
        out_specs=vmem,
        scratch_shapes=[
            pltpu.VMEM((PEERS, 32, PB), BF16),
            pltpu.VMEM((PEERS, 32, PB), BF16),
            pltpu.VMEM((NY * AD * BB, PB), BF16),
            pltpu.VMEM((OWN, AD * BB, PB), BF16),
            pltpu.VMEM((PEERS, PB), jnp.int32),
            pltpu.SMEM((PEERS, PB), jnp.int32),
            pltpu.VMEM((PEERS * OWN, 8, PB), F32),
            pltpu.VMEM((PEERS * OWN, 8, PB), F32),
            pltpu.VMEM((AD * BB, PEERS * PB), BF16),
            pltpu.VMEM((PEERS * PB, PB), BF16),
            pltpu.VMEM((OWN * AD * BB, PB), F32),
            pltpu.VMEM((NX, NY * NC, 4, PB), F32),
            pltpu.VMEM((PEERS * NC, 4, PB), F32),
            pltpu.VMEM((4, PB), F32),
            pltpu.VMEM((NZ, 4, PB), F32),
            pltpu.VMEM((4, PB), F32),
            pltpu.VMEM((NY * NC, 4, PB), F32),
            dma((PEERS,)), dma((PEERS,)),
            dma((NY,)), dma((NY,)),
            dma((NX,)), dma((3 * NX,)), dma((NX,)), dma((NX,)), dma((NX,)),
            dma((PEERS * NC,)), dma((PEERS * NC,)),
            dma((NZ,)), dma((NZ,)),
            dma((NY * NC,)), dma((NY * NC,)),
            dma((4,)),
        ],
        compiler_params=pltpu.CompilerParams(
            collective_id=0, has_side_effects=True, vmem_limit_bytes=32 * 1024 * 1024
        ),
    )(t, occ, virt, occ_column, partner_live)


def solution(mesh):
    placed = (
        P("wide", None, None),
        P("wide", "pair", None, None),
        P("wide", "pair", None, None),
        P("wide", "pair"),
        P("wide", "pair"),
    )
    return jax.shard_map(
        local, mesh=mesh, in_specs=placed, out_specs=P("pair", None), check_vma=False
    )
```

time: 794 us -> 60.7 us (0.08)
  waiting for transfers between devices: 438 us -> 0 us
  blocking collectives: 277 us -> 0 us
  Pallas kernels: 0 us -> 56.6 us
  local copies, waits for them, and re-layouts: 32.3 us -> 3.82 us
  starting transfers between devices: 21.2 us -> 0 us
  between operations: 13.6 us -> 0.01 us
    psum x1 -> x0, waiting for transfers between devices: 438 us -> none  [local(): total = lax.psum(response_part, ('wide', 'pair'))]
    all_gather x1 -> x0, blocking collectives: 277 us -> none  [local(): lax.all_gather(occ_column, 'wide', axis=0, tiled=True)]
    pallas_call x0 -> x1, Pallas kernels: none -> 56.6 us  [local(): pl.pallas_call(kernel, out_shape=jax.ShapeDtypeStruct((32, PB), F32), in_...]
    all_to_all x1 -> x0, starting transfers between devices: 21.2 us -> none  [local(): lax.all_to_all(outgoing.reshape(wide_count, CAP, block_size, wide_row), '...]
    scatter x1 -> x0, local copies, waits for them, and re-layouts: 15.7 us -> none  [local(): jnp.zeros((slot_total, block_size, wide_row), jnp.bfloat16).at[position]]
  transfers between devices with their start and end apart: 2 -> 0, of which waited for: 1 -> 0; matrix products, arithmetic and copies ran while one was open for 1% -> 0% of each run, Pallas kernels for 0% -> 0%
where the time goes in v1:
time: 60.7 us; the launch traced here: 60.4 us
  Pallas kernels  56.6 us (93%)
  local copies, waits for them, and re-layouts  3.82 us (6%)
    pallas_call x1, Pallas kernels, local(): pl.pallas_call(kernel, out_shape=jax.ShapeDtypeStruct((32, PB), F32), in_...  56.6 us
    unnamed x11, local copies, waits for them, and re-layouts  3.82 us

profile of v1, /device:TPU:1, one launch (start us, length us, event | category | flops | bytes accessed | tf_op | source)
XLA Modules:
  0.0 60.4 jit_solution(2267407568958856542)
XLA Ops:
  0.0 0.0 copy-start.4
  0.0 0.0 copy-start.3
  0.0 0.7 %copy-done.4 = s32[4,32]{1,0:T(4,128)S(1)} copy-done((s32[4,32]{1,0:T(4,128)S(1)}, s32[4,32]{1,0:T(4,128)}, u32[]{:S(2)}) %copy-start.4) | copy-done | bytes 536
  0.7 0.0 copy-done.3
  0.7 0.0 copy-start
  0.7 0.8 %copy-done = bf16[4,8,1024]{2,1,0:T(8,128)(2,1)S(1)} copy-done((bf16[4,8,1024]{2,1,0:T(8,128)(2,1)S(1)}, bf16[4,8,1024]{2,1,0:T(8,128)(2,1)}, u32[]{:S(2)}) %copy-start) | copy-done | bytes 65560
  1.5 0.0 copy-start.1
  1.5 0.8 %copy-done.1 = bf16[4,32,8,8]{1,3,2,0:T(8,128)(2,1)S(1)} copy-done((bf16[4,32,8,8]{1,3,2,0:T(8,128)(2,1)S(1)}, bf16[4,32,8,8]{1,3,2,0:T(8,128)(2,1)}, u32[]{:S(2)}) %copy-start.1) | copy-done | bytes 16408
  2.4 0.0 copy-start.2
  2.4 0.8 %copy-done.2 = bf16[4,32,8,8]{1,3,2,0:T(8,128)(2,1)S(1)} copy-done((bf16[4,32,8,8]{1,3,2,0:T(8,128)(2,1)S(1)}, bf16[4,32,8,8]{1,3,2,0:T(8,128)(2,1)}, u32[]{:S(2)}) %copy-start.2) | copy-done | bytes 16408
  3.2 56.6 %shard_map.55 = f32[32,128]{1,0:T(8,128)S(1)} custom-call(bf16[256,128]{1,0:T(8,128)(2,1)S(1)} %bitcast.11, bf16[4,64,32]{2,1,0:T(8,128)(2,1)S(1)} %bitcast.12, bf16[4,64,32]{2,1,0:T(8,128)(2,1)S(1)} %bitcast.13, s32[4,32]{1,0:T(4,128)S(1)} %copy-done.3, s32[4,32]{1,0:T(4,128)S(1)} %copy-done.4), custom_call_target="tpu_custom_call" | custom-call | tf_op jit(solution)/shard_map/pallas_call | solution.py:299
  59.8 0.6 %copy.7 = f32[32,128]{1,0:T(8,128)} copy(f32[32,128]{1,0:T(8,128)S(1)} %shard_map.55) | data formatting | bytes 32768
Async XLA Ops:
  0.0 0.7 %copy-start.4 = (s32[4,32]{1,0:T(4,128)S(1)}, s32[4,32]{1,0:T(4,128)}, u32[]{:S(2)}) copy-start(s32[4,32]{1,0:T(4,128)} %live_ref.1) | copy-start | bytes 1540
  0.0 0.7 %copy-start.3 = (s32[4,32]{1,0:T(4,128)S(1)}, s32[4,32]{1,0:T(4,128)}, u32[]{:S(2)}) copy-start(s32[4,32]{1,0:T(4,128)} %col_ref.1) | copy-start | bytes 1540
  0.7 0.8 %copy-start = (bf16[4,8,1024]{2,1,0:T(8,128)(2,1)S(1)}, bf16[4,8,1024]{2,1,0:T(8,128)(2,1)}, u32[]{:S(2)}) copy-start(bf16[4,8,1024]{2,1,0:T(8,128)(2,1)} %param.5) | copy-start | bytes 196612
  1.5 0.8 %copy-start.1 = (bf16[4,32,8,8]{1,3,2,0:T(8,128)(2,1)S(1)}, bf16[4,32,8,8]{1,3,2,0:T(8,128)(2,1)}, u32[]{:S(2)}) copy-start(bf16[4,32,8,8]{1,3,2,0:T(8,128)(2,1)} %param.6) | copy-start | bytes 49156
  2.4 0.8 %copy-start.2 = (bf16[4,32,8,8]{1,3,2,0:T(8,128)(2,1)S(1)}, bf16[4,32,8,8]{1,3,2,0:T(8,128)(2,1)}, u32[]{:S(2)}) copy-start(bf16[4,32,8,8]{1,3,2,0:T(8,128)(2,1)} %param.7) | copy-start | bytes 49156

commit v2 on v1

--- a/solution.py
+++ b/solution.py
@@ -28,8 +28,8 @@
 
 
 def kernel(
-    t_ref, occ_ref, virt_ref, col_ref, live_ref, out_ref,
-    sbuf, rbuf, ta, tk, meta_v, meta_s, oo, vv, lhs, rhs, yb, r3, g1, mine, g2, fin, g3,
+    t_hbm, occ_hbm, virt_hbm, col_hbm, live_hbm, out_ref,
+    occ_ref, virt_ref, col_ref, live_ref, sbuf, rbuf, ta, tk, meta_v, meta_s, oo, vv, lhs, rhs, yb, r3, g1, mine, g2, fin, g3,
     u_send, u_recv, a_send, a_recv, ka_send, kb_send, kc_send, k_recv, kc_recv,
     p1_send, p1_recv, p2_send, p2_recv, p3_send, p3_recv, loc,
 ):
@@ -47,22 +47,26 @@
             src_ref=src, dst_ref=dst, send_sem=ss, recv_sem=rs, device_id=(wide, pair), device_id_type=MESH
         )
 
+    t_ref = ta.at[pl.ds(0, AD * BB)]
+    load_t = pltpu.make_async_copy(t_hbm, t_ref, loc.at[0])
+    loads = [
+        pltpu.make_async_copy(src, dst, loc.at[4 + n])
+        for n, (src, dst) in enumerate(
+            ((col_hbm, col_ref), (live_hbm, live_ref), (occ_hbm, occ_ref), (virt_hbm, virt_ref))
+        )
+    ]
+    for copy in loads:
+        copy.start()
+    load_t.start()
+
+    greeted = [(z, (y + dy) % NY, c, (x + dx) % NX) for dx in range(NX) for dy in range(NY) if dx + dy]
+    greeted += [(z, y, 1 - c, x)]
+    greeted += [((z + dz) % NZ, y, c, x) for dz in (1, NZ - 1, 2, NZ - 2, NX, NZ - NX)]
     barrier = pltpu.get_barrier_semaphore()
-    for dx in range(NX):
-        for dy in range(NY):
-            for dc in range(NC):
-                if dx + dy + dc:
-                    pl.semaphore_signal(
-                        barrier, inc=1, device_id_type=MESH,
-                        device_id=(place(z, (y + dy) % NY, (c + dc) % NC), (x + dx) % NX),
-                    )
-    for dz in range(1, NZ):
-        pl.semaphore_signal(
-            barrier, inc=1, device_id_type=MESH, device_id=(place((z + dz) % NZ, y, c), x)
-        )
-
-    own_ta = pltpu.make_async_copy(t_ref, ta.at[pl.ds(0, AD * BB)], loc.at[0])
-    own_ta.start()
+    for zz, yy, cc, xx in greeted:
+        pl.semaphore_signal(barrier, inc=1, device_id=(place(zz, yy, cc), xx), device_id_type=MESH)
+    for copy in loads:
+        copy.wait()
 
     tri = one_hot(iota((32, 32), 0) < iota((32, 32), 1)).astype(BF16)
     base = jnp.zeros((PEERS * OWN, 1), F32)
@@ -90,7 +94,7 @@
         sbuf[j, 0:16, :] = packed[j * 16 : (j + 1) * 16].astype(BF16)
         sbuf[j, 16:32, :] = jnp.broadcast_to(codes[j : j + 1], (16, PB)).astype(BF16)
 
-    pl.semaphore_wait(barrier, PEERS * NC - 1 + NZ - 1)
+    pl.semaphore_wait(barrier, len(greeted))
 
     offsets = [(dx, dy) for dx in range(NX) for dy in range(NY)]
     sends = []
@@ -103,6 +107,7 @@
     own_units = pltpu.make_async_copy(sbuf.at[x * NY + y], rbuf.at[0], loc.at[1])
     own_units.start()
 
+    load_t.wait()
     arrivals = []
     for dy in range(1, NY):
         copy = remote(
@@ -113,32 +118,35 @@
         sends.append(copy)
 
     phase = (z + NZ - x) % NX
-    source = (z + NZ - jnp.where(phase == 3, -1, phase)) % NZ
-    qs = source // NX
-
-    def spread(i, src, to_z):
-        row = ((qs + NX - i) % NX) * NC + c
-        if to_z:
-            for n, dz in enumerate((1, NZ - 1, 2)):
-                remote(
-                    src, tk.at[row], kb_send.at[i * 3 + n], k_recv.at[i], place((z + dz) % NZ, y, c), x
-                ).start()
-        remote(src, tk.at[row], kc_send.at[i], kc_recv.at[i], place(z, y, 1 - c), x).start()
-
-    def block(i):
-        return tk.at[((qs + NX - i) % NX) * NC + c]
-
-    def other(i):
-        return tk.at[((qs + NX - i) % NX) * NC + 1 - c]
+    way = 1 - 2 * c
+    shift = jnp.where(phase == 2, 2 * way, jnp.where(phase == 3, -1, phase))
+    qs = ((z + NZ - shift) % NZ) // NX
+
+    def block(i, core=c):
+        return tk.at[((qs + NX - i) % NX) * NC + core]
+
+    def got_block(i):
+        remote(t_ref, block(i), ka_send.at[0], k_recv.at[i], w, x).wait_recv()
+
+    def to_z(src, dst, ss, rs, dz):
+        remote(src, dst, ss, rs, place((z + NZ + dz) % NZ, y, c), x).start()
+
+    def around(i, src):
+        for n, dz in enumerate((1, -1, 2 * way)):
+            to_z(src, block(i), kb_send.at[i * 3 + n], k_recv.at[i], dz)
+
+    def across(i, src):
+        remote(src, block(i), kc_send.at[i], kc_recv.at[i], place(z, y, 1 - c), x).start()
 
     own_tk = pltpu.make_async_copy(t_ref, block(0), loc.at[2])
 
     @pl.when(phase == 0)
     def _():
+        to_z(t_ref, block(0), ka_send.at[0], k_recv.at[1], NX)
+        to_z(t_ref, block(0), ka_send.at[1], k_recv.at[3], -NX)
+        around(0, t_ref)
+        across(0, t_ref)
         own_tk.start()
-        for i in range(1, NX):
-            remote(t_ref, block(0), ka_send.at[i], k_recv.at[i], place((z + NX * i) % NZ, y, c), x).start()
-        spread(0, t_ref, True)
 
     own_units.wait()
     for d in range(1, PEERS):
@@ -163,11 +171,14 @@
 
     @pl.when(phase == 0)
     def _():
-        for i in range(1, NX):
-            remote(t_ref, block(i), ka_send.at[i], k_recv.at[i], w, x).wait_recv()
-            spread(i, block(i), True)
-
-    own_ta.wait()
+        got_block(1)
+        got_block(3)
+        relay = block(1 + 2 * c)
+        to_z(relay, relay, ka_send.at[2], k_recv.at[2], NX * way)
+        for i in (1, 3):
+            around(i, block(i))
+            across(i, block(i))
+
     for copy in arrivals:
         copy.wait_recv()
 
@@ -198,20 +209,31 @@
 
     lax.fori_loop(0, OWN // 2, one_owner, 0)
 
+    @pl.when(phase == 0)
+    def _():
+        got_block(2)
+        around(2, block(2))
+        across(2, block(2))
+
     @pl.when(phase != 0)
     def _():
-        for i in range(NX):
-            remote(t_ref, block(i), ka_send.at[i], k_recv.at[i], w, x).wait_recv()
-            spread(i, block(i), False)
+        for i in (0, 1, 3):
+            got_block(i)
+            across(i, block(i))
 
     lax.fori_loop(OWN // 2, OWN, one_owner, 0)
 
+    @pl.when(phase != 0)
+    def _():
+        got_block(2)
+        across(2, block(2))
+
     @pl.when(phase == 0)
     def _():
         own_tk.wait()
 
     for i in range(NX):
-        remote(t_ref, other(i), kc_send.at[i], kc_recv.at[i], w, x).wait_recv()
+        remote(t_ref, block(i, 1 - c), kc_send.at[i], kc_recv.at[i], w, x).wait_recv()
 
     total = jnp.zeros((2 * PB, PB), F32)
     for ow in range(OWN):
@@ -284,8 +306,8 @@
 
     @pl.when(phase == 0)
     def _():
-        for i in range(1, NX):
-            remote(t_ref, block(i), ka_send.at[i], k_recv.at[i], w, x).wait_send()
+        for i in range(3):
+            remote(t_ref, block(0), ka_send.at[i], k_recv.at[0], w, x).wait_send()
         for i in range(3 * NX):
             remote(t_ref, block(0), kb_send.at[i], k_recv.at[0], w, x).wait_send()
 
@@ -299,9 +321,13 @@
     return pl.pallas_call(
         kernel,
         out_shape=jax.ShapeDtypeStruct((32, PB), F32),
-        in_specs=[vmem] * 5,
+        in_specs=[pl.BlockSpec(memory_space=pltpu.HBM)] * 5,
         out_specs=vmem,
         scratch_shapes=[
+            pltpu.VMEM((AD, BB, 32), BF16),
+            pltpu.VMEM((AD, BB, 32), BF16),
+            pltpu.VMEM((AD, 32), jnp.int32),
+            pltpu.VMEM((AD, 32), jnp.int32),
             pltpu.VMEM((PEERS, 32, PB), BF16),
             pltpu.VMEM((PEERS, 32, PB), BF16),
             pltpu.VMEM((NY * AD * BB, PB), BF16),
@@ -325,12 +351,12 @@
             dma((PEERS * NC,)), dma((PEERS * NC,)),
             dma((NZ,)), dma((NZ,)),
             dma((NY * NC,)), dma((NY * NC,)),
-            dma((4,)),
+            dma((8,)),
         ],
         compiler_params=pltpu.CompilerParams(
             collective_id=0, has_side_effects=True, vmem_limit_bytes=32 * 1024 * 1024
         ),
-    )(t, occ, virt, occ_column, partner_live)
+    )(*[pltpu.with_memory_space_constraint(v, pltpu.HBM) for v in (t, occ, virt, occ_column, partner_live)])
 
 
 def solution(mesh):

time: 60.7 us -> 52.5 us (0.86)
  Pallas kernels: 56.6 us -> 51.7 us
  local copies, waits for them, and re-layouts: 3.82 us -> 0.61 us
    pallas_call x1, Pallas kernels: 56.6 us -> 51.7 us  [local(): pl.pallas_call(kernel, out_shape=jax.ShapeDtypeStruct((32, PB), F32), in_...]
    unnamed x11 -> x1, local copies, waits for them, and re-layouts: 3.82 us -> 0.61 us
where the time goes in v2:
time: 52.5 us; the launch traced here: 52.4 us
  Pallas kernels  51.7 us (98%)
  local copies, waits for them, and re-layouts  0.61 us (1%)
    pallas_call x1, Pallas kernels, local(): pl.pallas_call(kernel, out_shape=jax.ShapeDtypeStruct((32, PB), F32), in_...  51.7 us

profile of v2, /device:TPU:1, one launch (start us, length us, event | category | flops | bytes accessed | tf_op | source)
XLA Modules:
  0.0 52.4 jit_solution(4044886980355620275)
XLA Ops:
  0.0 51.7 %shard_map.55 = f32[32,128]{1,0:T(8,128)S(1)} custom-call(bf16[256,128]{1,0:T(8,128)(2,1)} %bitcast.11, bf16[4,64,32]{2,1,0:T(8,128)(2,1)} %bitcast.12, bf16[4,64,32]{2,1,0:T(8,128)(2,1)} %bitcast.13, s32[4,32]{1,0:T(4,128)} %col_hbm.1, s32[4,32]{1,0:T(4,128)} %live_hbm.1), custom_call_target="tpu_custom_call" | custom-call | tf_op jit(solution)/shard_map/pallas_call | solution.py:321
  51.8 0.6 %copy.7 = f32[32,128]{1,0:T(8,128)} copy(f32[32,128]{1,0:T(8,128)S(1)} %shard_map.55) | data formatting | bytes 32768

commit v3 on v2

--- a/solution.py
+++ b/solution.py
@@ -14,6 +14,9 @@
 PB = 128
 MESH = pl.DeviceIdType.MESH
 F32 = jnp.float32
+FAR_FIRST = sorted(
+    ((dx, dy) for dx in range(NX) for dy in range(NY)), key=lambda o: -min(o[0], NX - o[0]) - min(o[1], NY - o[1])
+)
 BF16 = jnp.bfloat16
 NT = (((1,), (1,)), ((), ()))
 TN = (((0,), (0,)), ((), ()))
@@ -29,15 +32,24 @@
 
 def kernel(
     t_hbm, occ_hbm, virt_hbm, col_hbm, live_hbm, out_ref,
-    occ_ref, virt_ref, col_ref, live_ref, sbuf, rbuf, ta, tk, meta_v, meta_s, oo, vv, lhs, rhs, yb, r3, g1, mine, g2, fin, g3,
+    occ_ref, virt_ref, col_ref, live_ref, sbuf, rbuf, ta, tk, meta_v, meta_s, oo, vv, lhs0, lhs1, rhs0, rhs1, yb, r3, g1, mine, g2, fin, g3,
     u_send, u_recv, a_send, a_recv, ka_send, kb_send, kc_send, k_recv, kc_recv,
     p1_send, p1_recv, p2_send, p2_recv, p3_send, p3_recv, loc,
 ):
     w = lax.axis_index("wide")
     x = lax.axis_index("pair")
-    z = w // (NY * NC)
-    y = (w // NC) % NY
-    c = w % NC
+    z = w >> 3
+    y = (w >> 1) & 3
+    c = w & 1
+
+    def at_x(n):
+        return (x + n) & (NX - 1)
+
+    def at_y(n):
+        return (y + n) & (NY - 1)
+
+    def at_z(n):
+        return (z + NZ + n) & (NZ - 1)
 
     def place(zz, yy, cc):
         return zz * (NY * NC) + yy * NC + cc
@@ -59,12 +71,48 @@
         copy.start()
     load_t.start()
 
-    greeted = [(z, (y + dy) % NY, c, (x + dx) % NX) for dx in range(NX) for dy in range(NY) if dx + dy]
+    greeted = [(at_z(dz), y, c, x) for dz in (NX, -NX)]
+    greeted += [(z, at_y(dy), c, at_x(dx)) for dx, dy in FAR_FIRST if dx + dy]
+    greeted += [(at_z(dz), y, c, x) for dz in (2, -2, 1, -1)]
     greeted += [(z, y, 1 - c, x)]
-    greeted += [((z + dz) % NZ, y, c, x) for dz in (1, NZ - 1, 2, NZ - 2, NX, NZ - NX)]
     barrier = pltpu.get_barrier_semaphore()
     for zz, yy, cc, xx in greeted:
         pl.semaphore_signal(barrier, inc=1, device_id=(place(zz, yy, cc), xx), device_id_type=MESH)
+    load_t.wait()
+    pl.semaphore_wait(barrier, len(greeted))
+    sends = []
+
+    phase = (z + NZ - x) & (NX - 1)
+    way = 1 - 2 * c
+    shift = jnp.where(phase == 2, 2 * way, jnp.where(phase == 3, -1, phase))
+    qs = at_z(-shift) >> 2
+
+    def block(i, core=c):
+        return tk.at[((qs + NX - i) & (NX - 1)) * NC + core]
+
+    def got_block(i):
+        remote(t_ref, block(i), ka_send.at[0], k_recv.at[i], w, x).wait_recv()
+
+    def to_z(src, dst, ss, rs, dz):
+        remote(src, dst, ss, rs, place(at_z(dz), y, c), x).start()
+
+    def around(i, src):
+        for n, dz in enumerate((1, -1, 2 * way)):
+            to_z(src, block(i), kb_send.at[i * 3 + n], k_recv.at[i], dz)
+
+    def across(i, src):
+        remote(src, block(i), kc_send.at[i], kc_recv.at[i], place(z, y, 1 - c), x).start()
+
+    own_tk = pltpu.make_async_copy(t_ref, block(0), loc.at[2])
+
+    @pl.when(phase == 0)
+    def _():
+        to_z(t_ref, block(0), ka_send.at[0], k_recv.at[1], NX)
+        to_z(t_ref, block(0), ka_send.at[1], k_recv.at[3], -NX)
+        around(0, t_ref)
+        across(0, t_ref)
+        own_tk.start()
+
     for copy in loads:
         copy.wait()
 
@@ -94,59 +142,36 @@
         sbuf[j, 0:16, :] = packed[j * 16 : (j + 1) * 16].astype(BF16)
         sbuf[j, 16:32, :] = jnp.broadcast_to(codes[j : j + 1], (16, PB)).astype(BF16)
 
-    pl.semaphore_wait(barrier, len(greeted))
-
     offsets = [(dx, dy) for dx in range(NX) for dy in range(NY)]
-    sends = []
-    for d, (dx, dy) in enumerate(offsets):
+    for dx, dy in FAR_FIRST:
+        d = dx * NY + dy
         if d:
-            xt, yt = (x + dx) % NX, (y + dy) % NY
+            xt, yt = at_x(dx), at_y(dy)
             copy = remote(sbuf.at[xt * NY + yt], rbuf.at[d], u_send.at[d], u_recv.at[d], place(z, yt, c), xt)
             copy.start()
             sends.append(copy)
     own_units = pltpu.make_async_copy(sbuf.at[x * NY + y], rbuf.at[0], loc.at[1])
     own_units.start()
 
-    load_t.wait()
     arrivals = []
-    for dy in range(1, NY):
+    for dy in (2, 1, 3):
         copy = remote(
-            t_ref, ta.at[pl.ds(dy * AD * BB, AD * BB)], a_send.at[dy], a_recv.at[dy], place(z, (y + dy) % NY, c), x
+            t_ref, ta.at[pl.ds(dy * AD * BB, AD * BB)], a_send.at[dy], a_recv.at[dy], place(z, at_y(dy), c), x
         )
         copy.start()
         arrivals.append(copy)
         sends.append(copy)
 
-    phase = (z + NZ - x) % NX
-    way = 1 - 2 * c
-    shift = jnp.where(phase == 2, 2 * way, jnp.where(phase == 3, -1, phase))
-    qs = ((z + NZ - shift) % NZ) // NX
-
-    def block(i, core=c):
-        return tk.at[((qs + NX - i) % NX) * NC + core]
-
-    def got_block(i):
-        remote(t_ref, block(i), ka_send.at[0], k_recv.at[i], w, x).wait_recv()
-
-    def to_z(src, dst, ss, rs, dz):
-        remote(src, dst, ss, rs, place((z + NZ + dz) % NZ, y, c), x).start()
-
-    def around(i, src):
-        for n, dz in enumerate((1, -1, 2 * way)):
-            to_z(src, block(i), kb_send.at[i * 3 + n], k_recv.at[i], dz)
-
-    def across(i, src):
-        remote(src, block(i), kc_send.at[i], kc_recv.at[i], place(z, y, 1 - c), x).start()
-
-    own_tk = pltpu.make_async_copy(t_ref, block(0), loc.at[2])
-
-    @pl.when(phase == 0)
-    def _():
-        to_z(t_ref, block(0), ka_send.at[0], k_recv.at[1], NX)
-        to_z(t_ref, block(0), ka_send.at[1], k_recv.at[3], -NX)
-        around(0, t_ref)
-        across(0, t_ref)
-        own_tk.start()
+    @pl.when(phase == 0)
+    def _():
+        first = 1 + 2 * c
+        got_block(first)
+        to_z(block(first), block(first), ka_send.at[2], k_recv.at[2], NX * way)
+        around(first, block(first))
+        across(first, block(first))
+        got_block(NX - first)
+        around(NX - first, block(NX - first))
+        across(NX - first, block(NX - first))
 
     own_units.wait()
     for d in range(1, PEERS):
@@ -169,45 +194,8 @@
             arr[:, g, :] = jnp.dot(both, sel, preferred_element_type=F32)
     to_smem.wait()
 
-    @pl.when(phase == 0)
-    def _():
-        got_block(1)
-        got_block(3)
-        relay = block(1 + 2 * c)
-        to_z(relay, relay, ka_send.at[2], k_recv.at[2], NX * way)
-        for i in (1, 3):
-            around(i, block(i))
-            across(i, block(i))
-
     for copy in arrivals:
         copy.wait_recv()
-
-    def one_owner(ow, carry):
-        low = iota((8, PB), 1) < BB
-        for d, (dx, dy) in enumerate(offsets):
-            c0, c1 = meta_s[d, ow], meta_s[d, OWN + ow]
-            kv = jnp.where(low, c0 & 3, c1 & 3)
-            o = oo[d * OWN + ow]
-            v = vv[d * OWN + ow]
-            vs = [jnp.broadcast_to(v[s : s + 1, :], (8, PB)) for s in range(8)]
-            for kk in range(AD):
-                ok = jnp.where(kv == kk, o, 0.0)
-                for s in range(0, 8, 2):
-                    m = jnp.concatenate([ok * vs[s], ok * vs[s + 1]], axis=0).astype(BF16)
-                    lhs[kk * BB + s * 8 : kk * BB + s * 8 + 16, d * PB : (d + 1) * PB] = m
-            for cap, code in ((0, c0), (1, c1)):
-                atoms = [ta[(dy * AD + a) * BB : (dy * AD + a + 1) * BB, :] for a in range(AD)]
-                low_pair = jnp.where((code & 4) == 0, atoms[0], atoms[1])
-                high_pair = jnp.where((code & 4) == 0, atoms[2], atoms[3])
-                rhs[d * PB + cap * BB : d * PB + (cap + 1) * BB, :] = jnp.where(
-                    (code & 8) == 0, low_pair, high_pair
-                )
-        yb[pl.ds(pl.multiple_of(ow * AD * BB, AD * BB), AD * BB), :] = jnp.dot(
-            lhs[...], rhs[...], preferred_element_type=F32
-        )
-        return carry
-
-    lax.fori_loop(0, OWN // 2, one_owner, 0)
 
     @pl.when(phase == 0)
     def _():
@@ -215,18 +203,54 @@
         around(2, block(2))
         across(2, block(2))
 
+    def build(ow, lhs, rhs):
+        low = iota((8, PB), 1) < BB
+        for dy in range(NY):
+            atoms = [ta[(dy * AD + a) * BB : (dy * AD + a + 1) * BB, :] for a in range(AD)]
+            for dx in range(NX):
+                d = dx * NY + dy
+                c0, c1 = meta_s[d, ow], meta_s[d, OWN + ow]
+                kv = jnp.where(low, c0 & 3, c1 & 3)
+                o = oo[d * OWN + ow]
+                v = vv[d * OWN + ow]
+                wide_v = [
+                    jnp.concatenate([jnp.broadcast_to(v[s + n : s + n + 1, :], (8, PB)) for n in range(2)], axis=0)
+                    for s in range(0, 8, 2)
+                ]
+                wide_v = [t.astype(BF16) for t in wide_v]
+                for kk in range(AD):
+                    ok = jnp.where(kv == kk, o, 0.0)
+                    ok = jnp.concatenate([ok, ok], axis=0).astype(BF16)
+                    for n, t in enumerate(wide_v):
+                        lhs[kk * BB + n * 16 : kk * BB + n * 16 + 16, d * PB : (d + 1) * PB] = ok * t
+                for cap, code in ((0, c0), (1, c1)):
+                    low_pair = jnp.where((code & 4) == 0, atoms[0], atoms[1])
+                    high_pair = jnp.where((code & 4) == 0, atoms[2], atoms[3])
+                    rhs[d * PB + cap * BB : d * PB + (cap + 1) * BB, :] = jnp.where(
+                        (code & 8) == 0, low_pair, high_pair
+                    )
+
+    def multiply(ow, lhs, rhs):
+        yb[pl.ds(pl.multiple_of(ow * AD * BB, AD * BB), AD * BB), :] = jnp.dot(
+            lhs[...], rhs[...], preferred_element_type=F32
+        )
+
+    def two_owners(n, carry):
+        multiply((2 * n + OWN - 1) & (OWN - 1), lhs1, rhs1)
+        build(2 * n, lhs0, rhs0)
+        multiply(2 * n, lhs0, rhs0)
+        build(2 * n + 1, lhs1, rhs1)
+        return carry
+
+    lax.fori_loop(0, OWN // 2, two_owners, 0)
+
     @pl.when(phase != 0)
     def _():
-        for i in (0, 1, 3):
+        for i in (0, 1, 3, 2):
             got_block(i)
             across(i, block(i))
 
-    lax.fori_loop(OWN // 2, OWN, one_owner, 0)
-
-    @pl.when(phase != 0)
-    def _():
-        got_block(2)
-        across(2, block(2))
+    multiply(OWN - 1, lhs1, rhs1)
 
     @pl.when(phase == 0)
     def _():
@@ -249,18 +273,14 @@
             r3[xx, n] = part[xx * 32 + n * 4 : xx * 32 + n * 4 + 4]
 
     waits = []
-    d = 0
-    for dx in range(NX):
-        for dy in range(NY):
-            for dc in range(NC):
-                if d:
-                    xt, yt, ct = (x + dx) % NX, (y + dy) % NY, (c + dc) % NC
-                    copy = remote(
-                        r3.at[xt, yt * NC + ct], g1.at[d], p1_send.at[d], p1_recv.at[d], place(z, yt, ct), xt
-                    )
-                    copy.start()
-                    waits.append(copy)
-                d += 1
+    for dx, dy in FAR_FIRST:
+        for dc in (1, 0):
+            d = (dx * NY + dy) * NC + dc
+            if d:
+                xt, yt, ct = at_x(dx), at_y(dy), c ^ dc
+                copy = remote(r3.at[xt, yt * NC + ct], g1.at[d], p1_send.at[d], p1_recv.at[d], place(z, yt, ct), xt)
+                copy.start()
+                waits.append(copy)
     total4 = r3[x, y * NC + c]
     for copy in waits:
         copy.wait_recv()
@@ -270,14 +290,25 @@
     mine[...] = total4
 
     waits = []
-    for dz in range(1, NZ):
-        copy = remote(mine, g2.at[z], p2_send.at[dz], p2_recv.at[dz], place((z + dz) % NZ, y, c), x)
+    for dz in sorted(range(1, NZ), key=lambda n: -min(n, NZ - n)):
+        copy = remote(mine, g2.at[z], p2_send.at[dz], p2_recv.at[dz], place(at_z(dz), y, c), x)
         copy.start()
         waits.append(copy)
     g2[z] = total4
+    for copy in sends:
+        copy.wait_send()
+    for i in range(NX):
+        remote(t_ref, block(i), kc_send.at[i], kc_recv.at[i], w, x).wait_send()
+
+    @pl.when(phase == 0)
+    def _():
+        for i in range(3):
+            remote(t_ref, block(0), ka_send.at[i], k_recv.at[0], w, x).wait_send()
+        for i in range(3 * NX):
+            remote(t_ref, block(0), kb_send.at[i], k_recv.at[0], w, x).wait_send()
     for copy in waits:
         copy.wait_recv()
-    sends += waits
+    sends = waits
     total4 = g2[0]
     for n in range(1, NZ):
         total4 += g2[n]
@@ -285,31 +316,23 @@
 
     waits = []
     here = y * NC + c
-    for n in range(1, NY * NC):
+    for n in (4, 5, 2, 3, 6, 7, 1):
         dy, dc = n // NC, n % NC
         copy = remote(
-            fin, g3.at[here], p3_send.at[n], p3_recv.at[n], place(z, (y + dy) % NY, (c + dc) % NC), x
+            fin, g3.at[here], p3_send.at[n], p3_recv.at[n], place(z, at_y(dy), c ^ dc), x
         )
         copy.start()
         waits.append(copy)
     g3[here] = total4
+    for copy in sends:
+        copy.wait_send()
     for copy in waits:
         copy.wait_recv()
-    sends += waits
     for n in range(NY * NC):
         out_ref[n * 4 : (n + 1) * 4, :] = g3[n]
 
-    for copy in sends:
+    for copy in waits:
         copy.wait_send()
-    for i in range(NX):
-        remote(t_ref, block(i), kc_send.at[i], kc_recv.at[i], w, x).wait_send()
-
-    @pl.when(phase == 0)
-    def _():
-        for i in range(3):
-            remote(t_ref, block(0), ka_send.at[i], k_recv.at[0], w, x).wait_send()
-        for i in range(3 * NX):
-            remote(t_ref, block(0), kb_send.at[i], k_recv.at[0], w, x).wait_send()
 
 
 def local(three_center, occ_green, virt_green, occ_column, partner_live):
@@ -337,6 +360,8 @@
             pltpu.VMEM((PEERS * OWN, 8, PB), F32),
             pltpu.VMEM((PEERS * OWN, 8, PB), F32),
             pltpu.VMEM((AD * BB, PEERS * PB), BF16),
+            pltpu.VMEM((AD * BB, PEERS * PB), BF16),
+            pltpu.VMEM((PEERS * PB, PB), BF16),
             pltpu.VMEM((PEERS * PB, PB), BF16),
             pltpu.VMEM((OWN * AD * BB, PB), F32),
             pltpu.VMEM((NX, NY * NC, 4, PB), F32),

time: 52.5 us -> 49.8 us (0.949)
  Pallas kernels: 51.7 us -> 49.1 us
    pallas_call x1, Pallas kernels: 51.7 us -> 49.1 us  [local(): pl.pallas_call(kernel, out_shape=jax.ShapeDtypeStruct((32, PB), F32), in_...]
where the time goes in v3:
time: 49.8 us; the launch traced here: 49.7 us
  Pallas kernels  49.1 us (99%)
  local copies, waits for them, and re-layouts  0.61 us (1%)
    pallas_call x1, Pallas kernels, local(): pl.pallas_call(kernel, out_shape=jax.ShapeDtypeStruct((32, PB), F32), in_...  49.1 us

profile of v3, /device:TPU:1, one launch (start us, length us, event | category | flops | bytes accessed | tf_op | source)
XLA Modules:
  0.0 49.7 jit_solution(13497478946670279691)
XLA Ops:
  0.0 49.1 %shard_map.55 = f32[32,128]{1,0:T(8,128)S(1)} custom-call(bf16[256,128]{1,0:T(8,128)(2,1)} %bitcast.11, bf16[4,64,32]{2,1,0:T(8,128)(2,1)} %bitcast.12, bf16[4,64,32]{2,1,0:T(8,128)(2,1)} %bitcast.13, s32[4,32]{1,0:T(4,128)} %col_hbm.1, s32[4,32]{1,0:T(4,128)} %live_hbm.1), custom_call_target="tpu_custom_call" | custom-call | tf_op jit(solution)/shard_map/pallas_call | solution.py:344
  49.1 0.6 %copy.7 = f32[32,128]{1,0:T(8,128)} copy(f32[32,128]{1,0:T(8,128)S(1)} %shard_map.55) | data formatting | bytes 32768

commit v4 on v3

--- a/solution.py
+++ b/solution.py
@@ -73,7 +73,7 @@
 
     greeted = [(at_z(dz), y, c, x) for dz in (NX, -NX)]
     greeted += [(z, at_y(dy), c, at_x(dx)) for dx, dy in FAR_FIRST if dx + dy]
-    greeted += [(at_z(dz), y, c, x) for dz in (2, -2, 1, -1)]
+    greeted += [(at_z(dz), y, c, x) for dz in (3, -3, 2, -2, 1, -1)]
     greeted += [(z, y, 1 - c, x)]
     barrier = pltpu.get_barrier_semaphore()
     for zz, yy, cc, xx in greeted:
@@ -83,9 +83,7 @@
     sends = []
 
     phase = (z + NZ - x) & (NX - 1)
-    way = 1 - 2 * c
-    shift = jnp.where(phase == 2, 2 * way, jnp.where(phase == 3, -1, phase))
-    qs = at_z(-shift) >> 2
+    qs = at_z(-phase) >> 2
 
     def block(i, core=c):
         return tk.at[((qs + NX - i) & (NX - 1)) * NC + core]
@@ -96,9 +94,9 @@
     def to_z(src, dst, ss, rs, dz):
         remote(src, dst, ss, rs, place(at_z(dz), y, c), x).start()
 
-    def around(i, src):
-        for n, dz in enumerate((1, -1, 2 * way)):
-            to_z(src, block(i), kb_send.at[i * 3 + n], k_recv.at[i], dz)
+    def beside(src, dst, first, i, side):
+        for n in range(3):
+            to_z(src, dst, kb_send.at[first + n], k_recv.at[i], side * (n + 1))
 
     def across(i, src):
         remote(src, block(i), kc_send.at[i], kc_recv.at[i], place(z, y, 1 - c), x).start()
@@ -109,7 +107,8 @@
     def _():
         to_z(t_ref, block(0), ka_send.at[0], k_recv.at[1], NX)
         to_z(t_ref, block(0), ka_send.at[1], k_recv.at[3], -NX)
-        around(0, t_ref)
+        beside(t_ref, block(0), 0, 0, 1)
+        beside(t_ref, block(0), 3, 3, -1)
         across(0, t_ref)
         own_tk.start()
 
@@ -164,14 +163,22 @@
 
     @pl.when(phase == 0)
     def _():
-        first = 1 + 2 * c
-        got_block(first)
-        to_z(block(first), block(first), ka_send.at[2], k_recv.at[2], NX * way)
-        around(first, block(first))
-        across(first, block(first))
-        got_block(NX - first)
-        around(NX - first, block(NX - first))
-        across(NX - first, block(NX - first))
+        got_block(1)
+
+        @pl.when(c == 0)
+        def _():
+            to_z(block(1), block(1), ka_send.at[2], k_recv.at[2], NX)
+
+        beside(block(1), block(1), 6, 1, 1)
+        across(1, block(1))
+        got_block(3)
+
+        @pl.when(c == 1)
+        def _():
+            to_z(block(3), block(3), ka_send.at[2], k_recv.at[2], -NX)
+
+        beside(block(3), block(3), 9, 2, -1)
+        across(3, block(3))
 
     own_units.wait()
     for d in range(1, PEERS):
@@ -196,12 +203,6 @@
 
     for copy in arrivals:
         copy.wait_recv()
-
-    @pl.when(phase == 0)
-    def _():
-        got_block(2)
-        around(2, block(2))
-        across(2, block(2))
 
     def build(ow, lhs, rhs):
         low = iota((8, PB), 1) < BB
@@ -246,9 +247,12 @@
 
     @pl.when(phase != 0)
     def _():
-        for i in (0, 1, 3, 2):
+        for i in (0, 3, 1):
             got_block(i)
             across(i, block(i))
+
+    got_block(2)
+    across(2, block(2))
 
     multiply(OWN - 1, lhs1, rhs1)
 

time: 49.8 us -> 47.2 us (0.948)
  Pallas kernels: 49.1 us -> 46.4 us
    pallas_call x1, Pallas kernels: 49.1 us -> 46.4 us  [local(): pl.pallas_call(kernel, out_shape=jax.ShapeDtypeStruct((32, PB), F32), in_...]
where the time goes in v4:
time: 47.2 us; the launch traced here: 47.1 us
  Pallas kernels  46.4 us (98%)
  local copies, waits for them, and re-layouts  0.61 us (1%)
    pallas_call x1, Pallas kernels, local(): pl.pallas_call(kernel, out_shape=jax.ShapeDtypeStruct((32, PB), F32), in_...  46.4 us

profile of v4, /device:TPU:1, one launch (start us, length us, event | category | flops | bytes accessed | tf_op | source)
XLA Modules:
  0.0 47.1 jit_solution(687149536251556560)
XLA Ops:
  0.0 46.4 %shard_map.55 = f32[32,128]{1,0:T(8,128)S(1)} custom-call(bf16[256,128]{1,0:T(8,128)(2,1)} %bitcast.11, bf16[4,64,32]{2,1,0:T(8,128)(2,1)} %bitcast.12, bf16[4,64,32]{2,1,0:T(8,128)(2,1)} %bitcast.13, s32[4,32]{1,0:T(4,128)} %col_hbm.1, s32[4,32]{1,0:T(4,128)} %live_hbm.1), custom_call_target="tpu_custom_call" | custom-call | tf_op jit(solution)/shard_map/pallas_call | solution.py:348
  46.5 0.6 %copy.7 = f32[32,128]{1,0:T(8,128)} copy(f32[32,128]{1,0:T(8,128)S(1)} %shard_map.55) | data formatting | bytes 32768

commit v5 on v4

--- a/solution.py
+++ b/solution.py
@@ -95,7 +95,7 @@
         remote(src, dst, ss, rs, place(at_z(dz), y, c), x).start()
 
     def beside(src, dst, first, i, side):
-        for n in range(3):
+        for n in (2, 1, 0):
             to_z(src, dst, kb_send.at[first + n], k_recv.at[i], side * (n + 1))
 
     def across(i, src):
@@ -204,43 +204,42 @@
     for copy in arrivals:
         copy.wait_recv()
 
-    def build(ow, lhs, rhs):
+    def build(ow, lhs, rhs, d):
         low = iota((8, PB), 1) < BB
-        for dy in range(NY):
-            atoms = [ta[(dy * AD + a) * BB : (dy * AD + a + 1) * BB, :] for a in range(AD)]
-            for dx in range(NX):
-                d = dx * NY + dy
-                c0, c1 = meta_s[d, ow], meta_s[d, OWN + ow]
-                kv = jnp.where(low, c0 & 3, c1 & 3)
-                o = oo[d * OWN + ow]
-                v = vv[d * OWN + ow]
-                wide_v = [
-                    jnp.concatenate([jnp.broadcast_to(v[s + n : s + n + 1, :], (8, PB)) for n in range(2)], axis=0)
-                    for s in range(0, 8, 2)
-                ]
-                wide_v = [t.astype(BF16) for t in wide_v]
-                for kk in range(AD):
-                    ok = jnp.where(kv == kk, o, 0.0)
-                    ok = jnp.concatenate([ok, ok], axis=0).astype(BF16)
-                    for n, t in enumerate(wide_v):
-                        lhs[kk * BB + n * 16 : kk * BB + n * 16 + 16, d * PB : (d + 1) * PB] = ok * t
-                for cap, code in ((0, c0), (1, c1)):
-                    low_pair = jnp.where((code & 4) == 0, atoms[0], atoms[1])
-                    high_pair = jnp.where((code & 4) == 0, atoms[2], atoms[3])
-                    rhs[d * PB + cap * BB : d * PB + (cap + 1) * BB, :] = jnp.where(
-                        (code & 8) == 0, low_pair, high_pair
-                    )
-
-    def multiply(ow, lhs, rhs):
-        yb[pl.ds(pl.multiple_of(ow * AD * BB, AD * BB), AD * BB), :] = jnp.dot(
-            lhs[...], rhs[...], preferred_element_type=F32
-        )
+        dy = d % NY
+        c0, c1 = meta_s[d, ow], meta_s[d, OWN + ow]
+        kv = jnp.where(low, c0 & 3, c1 & 3)
+        o = oo[d * OWN + ow]
+        v = vv[d * OWN + ow]
+        wide_v = [
+            jnp.concatenate([jnp.broadcast_to(v[s + n : s + n + 1, :], (8, PB)) for n in range(2)], axis=0)
+            for s in range(0, 8, 2)
+        ]
+        wide_v = [t.astype(BF16) for t in wide_v]
+        for kk in range(AD):
+            ok = jnp.where(kv == kk, o, 0.0)
+            ok = jnp.concatenate([ok, ok], axis=0).astype(BF16)
+            for n, t in enumerate(wide_v):
+                lhs[kk * BB + n * 16 : kk * BB + n * 16 + 16, d * PB : (d + 1) * PB] = ok * t
+        atoms = [ta[(dy * AD + a) * BB : (dy * AD + a + 1) * BB, :] for a in range(AD)]
+        for cap, code in ((0, c0), (1, c1)):
+            low_pair = jnp.where((code & 4) == 0, atoms[0], atoms[1])
+            high_pair = jnp.where((code & 4) == 0, atoms[2], atoms[3])
+            rhs[d * PB + cap * BB : d * PB + (cap + 1) * BB, :] = jnp.where((code & 8) == 0, low_pair, high_pair)
+
+    def multiply_and_build(done, lhs_done, rhs_done, ow, lhs, rhs):
+        total = jnp.zeros((AD * BB, PB), F32)
+        for d in range(0, PEERS, 2):
+            span = slice(d * PB, (d + 2) * PB)
+            total += jnp.dot(lhs_done[:, span], rhs_done[span, :], preferred_element_type=F32)
+            if ow is not None:
+                for n in range(2):
+                    build(ow, lhs, rhs, d + n)
+        yb[pl.ds(pl.multiple_of(done * AD * BB, AD * BB), AD * BB), :] = total
 
     def two_owners(n, carry):
-        multiply((2 * n + OWN - 1) & (OWN - 1), lhs1, rhs1)
-        build(2 * n, lhs0, rhs0)
-        multiply(2 * n, lhs0, rhs0)
-        build(2 * n + 1, lhs1, rhs1)
+        multiply_and_build((2 * n + OWN - 1) & (OWN - 1), lhs1, rhs1, 2 * n, lhs0, rhs0)
+        multiply_and_build(2 * n, lhs0, rhs0, 2 * n + 1, lhs1, rhs1)
         return carry
 
     lax.fori_loop(0, OWN // 2, two_owners, 0)
@@ -254,7 +253,7 @@
     got_block(2)
     across(2, block(2))
 
-    multiply(OWN - 1, lhs1, rhs1)
+    multiply_and_build(OWN - 1, lhs1, rhs1, None, None, None)
 
     @pl.when(phase == 0)
     def _():

time: 47.2 us -> 46.9 us (level)
  no operation moved by 1% of the time
where the time goes in v5:
time: 46.9 us; the launch traced here: 46.8 us
  Pallas kernels  46.2 us (99%)
  local copies, waits for them, and re-layouts  0.61 us (1%)
    pallas_call x1, Pallas kernels, local(): pl.pallas_call(kernel, out_shape=jax.ShapeDtypeStruct((32, PB), F32), in_...  46.2 us

profile of v5, /device:TPU:1, one launch (start us, length us, event | category | flops | bytes accessed | tf_op | source)
XLA Modules:
  0.0 46.8 jit_solution(17260098672877450099)
XLA Ops:
  0.0 46.2 %shard_map.55 = f32[32,128]{1,0:T(8,128)S(1)} custom-call(bf16[256,128]{1,0:T(8,128)(2,1)} %bitcast.11, bf16[4,64,32]{2,1,0:T(8,128)(2,1)} %bitcast.12, bf16[4,64,32]{2,1,0:T(8,128)(2,1)} %bitcast.13, s32[4,32]{1,0:T(4,128)} %col_hbm.1, s32[4,32]{1,0:T(4,128)} %live_hbm.1), custom_call_target="tpu_custom_call" | custom-call | tf_op jit(solution)/shard_map/pallas_call | solution.py:347
  46.2 0.6 %copy.7 = f32[32,128]{1,0:T(8,128)} copy(f32[32,128]{1,0:T(8,128)S(1)} %shard_map.55) | data formatting | bytes 32768

commit v6 on v5

--- a/solution.py
+++ b/solution.py
@@ -32,7 +32,7 @@
 
 def kernel(
     t_hbm, occ_hbm, virt_hbm, col_hbm, live_hbm, out_ref,
-    occ_ref, virt_ref, col_ref, live_ref, sbuf, rbuf, ta, tk, meta_v, meta_s, oo, vv, lhs0, lhs1, rhs0, rhs1, yb, r3, g1, mine, g2, fin, g3,
+    occ_ref, virt_ref, col_ref, live_ref, sbuf, rbuf, ta, tk, meta_v, meta_s, sel, oo, vv, lhs0, lhs1, rhs0, rhs1, yb, r3, g1, mine, g2, fin, g3,
     u_send, u_recv, a_send, a_recv, ka_send, kb_send, kc_send, k_recv, kc_recv,
     p1_send, p1_recv, p2_send, p2_recv, p3_send, p3_recv, loc,
 ):
@@ -152,6 +152,14 @@
     own_units = pltpu.make_async_copy(sbuf.at[x * NY + y], rbuf.at[0], loc.at[1])
     own_units.start()
 
+    row = iota((CAP * PB, PB), 0)
+    lane = iota((CAP * PB, PB), 1)
+    for f in range(2):
+        pick = (lane % 8) if f == 0 else (lane // 8) % 8
+        target = (lane // BB) * PB + f * BB + pick * 8
+        for g in range(8):
+            sel[f * 8 + g] = one_hot(row == target + g).astype(BF16)
+
     arrivals = []
     for dy in (2, 1, 3):
         copy = remote(
@@ -191,14 +199,9 @@
     both = jnp.concatenate(
         [got[:, 0].reshape(PEERS * OWN, PB).astype(BF16), got[:, 1].reshape(PEERS * OWN, PB).astype(BF16)], axis=1
     )
-    row = iota((CAP * PB, PB), 0)
-    lane = iota((CAP * PB, PB), 1)
     for f, arr in enumerate((oo, vv)):
-        pick = (lane % 8) if f == 0 else (lane // 8) % 8
-        target = (lane // BB) * PB + f * BB + pick * 8
         for g in range(8):
-            sel = one_hot(row == target + g).astype(BF16)
-            arr[:, g, :] = jnp.dot(both, sel, preferred_element_type=F32)
+            arr[:, g, :] = jnp.dot(both, sel[f * 8 + g], preferred_element_type=F32)
     to_smem.wait()
 
     for copy in arrivals:
@@ -360,6 +363,7 @@
             pltpu.VMEM((OWN, AD * BB, PB), BF16),
             pltpu.VMEM((PEERS, PB), jnp.int32),
             pltpu.SMEM((PEERS, PB), jnp.int32),
+            pltpu.VMEM((16, CAP * PB, PB), BF16),
             pltpu.VMEM((PEERS * OWN, 8, PB), F32),
             pltpu.VMEM((PEERS * OWN, 8, PB), F32),
             pltpu.VMEM((AD * BB, PEERS * PB), BF16),

time: 46.9 us -> 46.9 us (level)
  no operation moved by 1% of the time
where the time goes in v6:
time: 46.9 us; the launch traced here: 46.7 us
  Pallas kernels  46.1 us (98%)
  local copies, waits for them, and re-layouts  0.61 us (1%)
    pallas_call x1, Pallas kernels, local(): pl.pallas_call(kernel, out_shape=jax.ShapeDtypeStruct((32, PB), F32), in_...  46.1 us

profile of v6, /device:TPU:1, one launch (start us, length us, event | category | flops | bytes accessed | tf_op | source)
XLA Modules:
  0.0 46.7 jit_solution(8353902003331597954)
XLA Ops:
  0.0 46.1 %shard_map.55 = f32[32,128]{1,0:T(8,128)S(1)} custom-call(bf16[256,128]{1,0:T(8,128)(2,1)} %bitcast.11, bf16[4,64,32]{2,1,0:T(8,128)(2,1)} %bitcast.12, bf16[4,64,32]{2,1,0:T(8,128)(2,1)} %bitcast.13, s32[4,32]{1,0:T(4,128)} %col_hbm.1, s32[4,32]{1,0:T(4,128)} %live_hbm.1), custom_call_target="tpu_custom_call" | custom-call | tf_op jit(solution)/shard_map/pallas_call | solution.py:350
  46.1 0.6 %copy.7 = f32[32,128]{1,0:T(8,128)} copy(f32[32,128]{1,0:T(8,128)S(1)} %shard_map.55) | data formatting | bytes 32768
